TPU v7x, 32 devices: a whole 2x2x4 slice. The times are simulated.
32 devices in a mesh: dp: 8 (over z, y), mp: 4 (over x, core).
Axes of the slice: x: 2, y: 2, z: 4, core: 2. Of those that a mesh axis runs over, the one named last changes fastest.
Arguments:
- tokens: bfloat16 [8192, 2048], P('dp'), may hold values from -6 to 6
- documents: int32 [8, 1024], P('dp'), may hold values from 0 to 3, never falling along the last dimension, each value on 1 to 512 neighbouring positions
- cotangent: bfloat16 [8192, 2048], P('dp'), may hold values from -6 to 6
- attn_gain: float32 [2048], P('dp'), may hold values from 0.5 to 1.5
- query_gain: float32 [128], P('dp'), may hold values from 1 to 2
- key_norm_scale: float32 [128], P('dp'), may hold values from 0.25 to 1.75
- query_weight: float32 [2048, 2048], P('dp', 'mp'), may hold values from -0.125 to 0.125
- key_projection: float32 [2048, 1024], P('dp', 'mp'), may hold values from -0.125 to 0.125
- value_projection: float32 [2048, 1024], P('dp', 'mp'), may hold values from -0.125 to 0.125
- output_weight: float32 [2048, 2048], P('mp', 'dp'), may hold values from -1 to 1
- mlp_gain: float32 [2048], P('dp'), may hold values from 0.5 to 1.5
- gate_weight: float32 [2048, 6144], P('dp', 'mp'), may hold values from -0.125 to 0.125
- up_weight: float32 [2048, 6144], P('dp', 'mp'), may hold values from -0.125 to 0.125
- down_weight: float32 [6144, 2048], P('mp', 'dp'), may hold values from -0.078125 to 0.078125
Outputs:
- layer_output: bfloat16 [8192, 2048], P(('dp', 'mp'))
- input_grad: float32 [8192, 2048], P(('dp', 'mp'))
- attn_gain_grad: float32 [2048], P('dp')
- query_gain_grad: float32 [128], P('dp')
- key_gain_grad: float32 [128], P('dp')
- query_weight_grad: float32 [2048, 2048], P('dp', 'mp')
- key_weight_grad: float32 [2048, 1024], P('dp', 'mp')
- value_weight_grad: float32 [2048, 1024], P('dp', 'mp')
- output_weight_grad: float32 [2048, 2048], P('mp', 'dp')
- mlp_gain_grad: float32 [2048], P('dp')
- gate_weight_grad: float32 [2048, 6144], P('dp', 'mp')
- up_weight_grad: float32 [2048, 6144], P('dp', 'mp')
- down_weight_grad: float32 [6144, 2048], P('mp', 'dp')
Inputs may be any that keep to these rules, and one draw needn't show every extreme that they name: `documents`: document numbers never fall along a sequence; each document holds 1 to 512 positions, and some document holds exactly 512.
All inputs are finite; a program needn't handle non-finite values.
Results may differ from a plain program's by a relative error of at most 0.023.
Values may be sent and summed in bfloat16 or wider, within the bound.
A program may use at most 256 MiB of HBM per device.

v0:
```python
import jax
import jax.numpy as jnp
from jax import lax
from jax.sharding import PartitionSpec as P

QUERY_HEADS = 16
KEY_VALUE_HEADS = 8
HEAD_WIDTH = 128
EPSILON = 1e-06
MASKED = -1e30


def doc_positions(documents):
    indices = jnp.arange(documents.shape[-1], dtype=jnp.int32)
    boundary = jnp.concatenate(
        [
            jnp.ones(documents.shape[:-1] + (1,), dtype=jnp.bool_),
            documents[:, 1:] != documents[:, :-1],
        ],
        -1,
    )
    starts = lax.cummax(jnp.where(boundary, indices[None, :], 0), axis=1)
    return indices[None, :] - starts


def rope_tables(positions, head_size):
    middle = head_size // 2
    frequency = jnp.power(1000000.0, -2.0 * jnp.arange(middle, dtype=jnp.float32) / head_size)
    angles = positions.astype(jnp.float32)[:, None] * frequency[None, :]
    cosine_table = jnp.cos(angles)
    sine_table = jnp.sin(angles)
    return (
        jnp.concatenate([cosine_table, cosine_table], -1),
        jnp.concatenate([sine_table, sine_table], -1),
    )


def rotate(values):
    middle = values.shape[-1] // 2
    return jnp.concatenate([-values[..., middle:], values[..., :middle]], -1)


def rotate_back(values):
    middle = values.shape[-1] // 2
    return jnp.concatenate([values[..., middle:], -values[..., :middle]], -1)


def norm_parts(values):
    scaling = lax.rsqrt(jnp.mean(values * values, -1, keepdims=True) + EPSILON)
    return (values * scaling, scaling)


def norm_back(grad_normed, normed_hat, scaling, gains):
    scaled = grad_normed * gains
    return scaling * (scaled - normed_hat * jnp.mean(scaled * normed_hat, -1, keepdims=True))


def contract_rows(left, right):
    return lax.dot_general(
        left, right, (((0,), (0,)), ((), ())), preferred_element_type=jnp.float32
    )


def contract_cols(left, right):
    return lax.dot_general(
        left, right, (((1,), (1,)), ((), ())), preferred_element_type=jnp.float32
    )


def block_scores(query_rows, key_token_rows, doc_row, start, width, factor):
    scores = (
        jnp.einsum("qgrd,kgd->grqk", query_rows, key_token_rows, preferred_element_type=jnp.float32)
        * factor
    )
    query_index = start + jnp.arange(width)
    key_index = jnp.arange(key_token_rows.shape[0])
    allowed = (doc_row[start : start + width, None] == doc_row[None, :]) & (
        key_index[None, :] <= query_index[:, None]
    )
    return jnp.where(allowed, scores, MASKED)


def on_device(
    tokens,
    documents,
    cotangent,
    attn_gain,
    query_gain,
    key_norm_scale,
    query_weight,
    key_projection,
    value_projection,
    output_weight,
    mlp_gain,
    gate_weight,
    up_weight,
    down_weight,
):
    rows = tokens.shape[0]
    seqs, seq_length = documents.shape
    head_size = HEAD_WIDTH
    local_heads = QUERY_HEADS // lax.axis_size("mp")
    device_groups = KEY_VALUE_HEADS // lax.axis_size("mp")
    query_group = QUERY_HEADS // KEY_VALUE_HEADS
    block = min(512, seq_length)
    factor = head_size ** (-0.5)
    share = rows // lax.axis_size("mp")
    offset = lax.axis_index("mp") * share

    def take(values):
        return lax.dynamic_slice_in_dim(values, offset, share, 0)

    attn_parts = (
        lax.all_gather(attn_gain.astype(jnp.bfloat16), "dp", axis=0, tiled=True),
        lax.all_gather(query_gain.astype(jnp.bfloat16), "dp", axis=0, tiled=True),
        lax.all_gather(key_norm_scale.astype(jnp.bfloat16), "dp", axis=0, tiled=True),
        lax.all_gather(query_weight.astype(jnp.bfloat16), "dp", axis=0, tiled=True),
        lax.all_gather(key_projection.astype(jnp.bfloat16), "dp", axis=0, tiled=True),
        lax.all_gather(value_projection.astype(jnp.bfloat16), "dp", axis=0, tiled=True),
        lax.all_gather(output_weight.astype(jnp.bfloat16), "dp", axis=1, tiled=True),
    )
    gain_one = attn_parts[0].astype(jnp.float32)
    gain_query = attn_parts[1].astype(jnp.float32)
    gain_key = attn_parts[2].astype(jnp.float32)
    query_mat, key_mat, value_mat, output_mat = (
        attn_parts[3],
        attn_parts[4],
        attn_parts[5],
        attn_parts[6],
    )
    mlp_parts = (
        lax.all_gather(mlp_gain.astype(jnp.bfloat16), "dp", axis=0, tiled=True),
        lax.all_gather(gate_weight.astype(jnp.bfloat16), "dp", axis=0, tiled=True),
        lax.all_gather(up_weight.astype(jnp.bfloat16), "dp", axis=0, tiled=True),
        lax.all_gather(down_weight.astype(jnp.bfloat16), "dp", axis=1, tiled=True),
    )
    gain_two = mlp_parts[0].astype(jnp.float32)
    gate_mat, up_mat, down_mat = (mlp_parts[1], mlp_parts[2], mlp_parts[3])
    inputs = tokens.astype(jnp.float32)
    hat_one, inv_one = norm_parts(inputs)
    normed_one = (hat_one * gain_one).astype(jnp.bfloat16)
    query_raw = jnp.dot(normed_one, query_mat, preferred_element_type=jnp.float32)
    key_unnormed = jnp.dot(normed_one, key_mat, preferred_element_type=jnp.float32)
    value_token_rows = jnp.dot(normed_one, value_mat, preferred_element_type=jnp.float32).astype(
        jnp.bfloat16
    )
    positions = doc_positions(documents).reshape(rows)
    cosine_table, sine_table = rope_tables(positions, head_size)
    cosine_table = cosine_table[:, None, :]
    sine_table = sine_table[:, None, :]
    query_hat, query_inv = norm_parts(query_raw.reshape(rows, local_heads, head_size))
    key_hat, key_inv = norm_parts(key_unnormed.reshape(rows, device_groups, head_size))
    query_normed = query_hat * gain_query
    key_normed = key_hat * gain_key
    query_rows = (query_normed * cosine_table + rotate(query_normed) * sine_table).astype(
        jnp.bfloat16
    )
    key_token_rows = (key_normed * cosine_table + rotate(key_normed) * sine_table).astype(
        jnp.bfloat16
    )
    query_seq = query_rows.reshape(seqs, seq_length, device_groups, query_group, head_size)
    key_seq = key_token_rows.reshape(seqs, seq_length, device_groups, head_size)
    value_seq = value_token_rows.reshape(seqs, seq_length, device_groups, head_size)

    def attend_forward(items):
        seq_queries, seq_keys, seq_values, doc_row = items
        outputs = []
        log_totals = []
        for start in range(0, seq_length, block):
            scores = block_scores(
                seq_queries[start : start + block], seq_keys, doc_row, start, block, factor
            )
            highest = jnp.max(scores, -1, keepdims=True)
            exponent = jnp.exp(scores - highest)
            totals = jnp.sum(exponent, -1, keepdims=True)
            weights_block = (exponent / totals).astype(jnp.bfloat16)
            outputs.append(
                jnp.einsum(
                    "grqk,kgd->qgrd", weights_block, seq_values, preferred_element_type=jnp.float32
                )
            )
            log_totals.append(highest + jnp.log(totals))
        return (jnp.concatenate(outputs, 0), jnp.concatenate(log_totals, 2))

    attention_output, log_total = lax.map(
        attend_forward, (query_seq, key_seq, value_seq, documents)
    )
    attended_flat = attention_output.reshape(rows, local_heads * head_size).astype(jnp.bfloat16)
    attn_part = jnp.dot(attended_flat, output_mat, preferred_element_type=jnp.float32)
    hidden = inputs + lax.psum(attn_part, "mp")
    hat_two, inv_two = norm_parts(hidden)
    normed_two = (hat_two * gain_two).astype(jnp.bfloat16)
    hidden_share = take(hidden)
    gate_pre = jnp.dot(normed_two, gate_mat, preferred_element_type=jnp.float32)
    up_pre = jnp.dot(normed_two, up_mat, preferred_element_type=jnp.float32)
    sigmoid = jax.nn.sigmoid(gate_pre)
    swish = gate_pre * sigmoid
    active = (swish * up_pre).astype(jnp.bfloat16)
    mlp_part = jnp.dot(active, down_mat, preferred_element_type=jnp.float32)
    layer_output = (
        hidden_share + take(lax.psum(mlp_part.astype(jnp.bfloat16), "mp").astype(jnp.float32))
    ).astype(jnp.bfloat16)
    back_gain_one, back_gain_query, back_gain_key = (gain_one, gain_query, gain_key)
    back_query, back_key, back_value, back_output = (query_mat, key_mat, value_mat, output_mat)
    back_gate, back_up, back_down = (gate_mat, up_mat, down_mat)
    grad_out = cotangent.astype(jnp.float32)
    grad_active = contract_cols(cotangent, back_down)
    down_grad = contract_rows(active, cotangent)
    grad_gate = (grad_active * up_pre * sigmoid * (1.0 + gate_pre * (1.0 - sigmoid))).astype(
        jnp.bfloat16
    )
    grad_up = (grad_active * swish).astype(jnp.bfloat16)
    gate_grad = contract_rows(normed_two, grad_gate)
    up_grad = contract_rows(normed_two, grad_up)
    normed_two_part = contract_cols(grad_gate, back_gate) + contract_cols(grad_up, back_up)
    normed_two_grad = lax.psum(normed_two_part.astype(jnp.bfloat16), "mp").astype(jnp.float32)
    mlp_gain_part = jnp.sum(normed_two_grad * hat_two, 0)
    grad_hidden = grad_out + norm_back(normed_two_grad, hat_two, inv_two, gain_two)
    grad_hidden_low = grad_hidden.astype(jnp.bfloat16)
    grad_hidden_share = take(grad_hidden)
    output_grad = contract_rows(attended_flat, grad_hidden_low)
    grad_attended = contract_cols(grad_hidden_low, back_output).astype(jnp.bfloat16)
    grad_attended_seq = grad_attended.reshape(
        seqs, seq_length, device_groups, query_group, head_size
    )

    def attend_backward(items):
        seq_queries, seq_keys, seq_values, doc_row, seq_log_total, seq_grad = items
        query_grads = []
        key_grad = jnp.zeros((seq_length, device_groups, head_size), jnp.float32)
        value_grad = jnp.zeros((seq_length, device_groups, head_size), jnp.float32)
        for start in range(0, seq_length, block):
            block_queries = seq_queries[start : start + block]
            block_grad = seq_grad[start : start + block]
            scores = block_scores(block_queries, seq_keys, doc_row, start, block, factor)
            weights_block = jnp.exp(scores - seq_log_total[:, :, start : start + block])
            grad_weights = jnp.einsum(
                "qgrd,kgd->grqk", block_grad, seq_values, preferred_element_type=jnp.float32
            )
            inner = jnp.sum(weights_block * grad_weights, -1, keepdims=True)
            grad_scores = (weights_block * (grad_weights - inner)).astype(jnp.bfloat16)
            query_grads.append(
                jnp.einsum(
                    "grqk,kgd->qgrd", grad_scores, seq_keys, preferred_element_type=jnp.float32
                )
                * factor
            )
            key_grad = (
                key_grad
                + jnp.einsum(
                    "grqk,qgrd->kgd", grad_scores, block_queries, preferred_element_type=jnp.float32
                )
                * factor
            )
            value_grad = value_grad + jnp.einsum(
                "grqk,qgrd->kgd",
                weights_block.astype(jnp.bfloat16),
                block_grad,
                preferred_element_type=jnp.float32,
            )
        return (jnp.concatenate(query_grads, 0), key_grad, value_grad)

    query_rot_grad, key_rot_grad, value_seq_grad = lax.map(
        attend_backward, (query_seq, key_seq, value_seq, documents, log_total, grad_attended_seq)
    )
    query_rot_grad = query_rot_grad.reshape(rows, local_heads, head_size)
    key_rot_grad = key_rot_grad.reshape(rows, device_groups, head_size)
    query_norm_grad = query_rot_grad * cosine_table + rotate_back(query_rot_grad * sine_table)
    key_norm_grad = key_rot_grad * cosine_table + rotate_back(key_rot_grad * sine_table)
    query_gain_part = jnp.sum(query_norm_grad * query_hat, (0, 1))
    key_gain_part = jnp.sum(key_norm_grad * key_hat, (0, 1))
    query_raw_grad = (
        norm_back(query_norm_grad, query_hat, query_inv, back_gain_query)
        .reshape(rows, local_heads * head_size)
        .astype(jnp.bfloat16)
    )
    key_raw_grad = (
        norm_back(key_norm_grad, key_hat, key_inv, back_gain_key)
        .reshape(rows, device_groups * head_size)
        .astype(jnp.bfloat16)
    )
    value_raw_grad = value_seq_grad.reshape(rows, device_groups * head_size).astype(jnp.bfloat16)
    query_grad = contract_rows(normed_one, query_raw_grad)
    key_grad = contract_rows(normed_one, key_raw_grad)
    value_grad = contract_rows(normed_one, value_raw_grad)
    normed_one_part = (
        contract_cols(query_raw_grad, back_query)
        + contract_cols(key_raw_grad, back_key)
        + contract_cols(value_raw_grad, back_value)
    )
    hat_one_share = take(hat_one)
    inv_one_share = take(inv_one)
    normed_one_grad, query_gain_sum, key_gain_sum = (
        lax.psum(normed_one_part.astype(jnp.bfloat16), "mp").astype(jnp.float32),
        lax.psum(query_gain_part.astype(jnp.bfloat16), "mp").astype(jnp.float32),
        lax.psum(key_gain_part.astype(jnp.bfloat16), "mp").astype(jnp.float32),
    )
    attn_gain_total = jnp.sum(normed_one_grad * hat_one, 0)
    input_grad = grad_hidden_share + norm_back(
        take(normed_one_grad), hat_one_share, inv_one_share, back_gain_one
    )
    attn_grads = (
        lax.psum_scatter(
            attn_gain_total.astype(jnp.bfloat16), "dp", scatter_dimension=0, tiled=True
        ).astype(jnp.float32),
        lax.psum_scatter(
            query_gain_sum.astype(jnp.bfloat16), "dp", scatter_dimension=0, tiled=True
        ).astype(jnp.float32),
        lax.psum_scatter(
            key_gain_sum.astype(jnp.bfloat16), "dp", scatter_dimension=0, tiled=True
        ).astype(jnp.float32),
        lax.psum_scatter(
            query_grad.astype(jnp.bfloat16), "dp", scatter_dimension=0, tiled=True
        ).astype(jnp.float32),
        lax.psum_scatter(
            key_grad.astype(jnp.bfloat16), "dp", scatter_dimension=0, tiled=True
        ).astype(jnp.float32),
        lax.psum_scatter(
            value_grad.astype(jnp.bfloat16), "dp", scatter_dimension=0, tiled=True
        ).astype(jnp.float32),
        lax.psum_scatter(
            output_grad.astype(jnp.bfloat16), "dp", scatter_dimension=1, tiled=True
        ).astype(jnp.float32),
    )
    mlp_grads = (
        lax.psum_scatter(
            mlp_gain_part.astype(jnp.bfloat16), "dp", scatter_dimension=0, tiled=True
        ).astype(jnp.float32),
        lax.psum_scatter(
            gate_grad.astype(jnp.bfloat16), "dp", scatter_dimension=0, tiled=True
        ).astype(jnp.float32),
        lax.psum_scatter(
            up_grad.astype(jnp.bfloat16), "dp", scatter_dimension=0, tiled=True
        ).astype(jnp.float32),
        lax.psum_scatter(
            down_grad.astype(jnp.bfloat16), "dp", scatter_dimension=1, tiled=True
        ).astype(jnp.float32),
    )
    return (
        layer_output,
        input_grad,
        attn_grads[0],
        attn_grads[1],
        attn_grads[2],
        attn_grads[3],
        attn_grads[4],
        attn_grads[5],
        attn_grads[6],
        mlp_grads[0],
        mlp_grads[1],
        mlp_grads[2],
        mlp_grads[3],
    )


def solution(mesh):
    in_specs = (
        P("dp", None),
        P("dp", None),
        P("dp", None),
        P("dp"),
        P("dp"),
        P("dp"),
        P("dp", "mp"),
        P("dp", "mp"),
        P("dp", "mp"),
        P("mp", "dp"),
        P("dp"),
        P("dp", "mp"),
        P("dp", "mp"),
        P("mp", "dp"),
    )
    out_specs = (
        P(("dp", "mp"), None),
        P(("dp", "mp"), None),
        P("dp"),
        P("dp"),
        P("dp"),
        P("dp", "mp"),
        P("dp", "mp"),
        P("dp", "mp"),
        P("mp", "dp"),
        P("dp"),
        P("dp", "mp"),
        P("dp", "mp"),
        P("mp", "dp"),
    )
    return jax.shard_map(
        on_device, mesh=mesh, in_specs=in_specs, out_specs=out_specs, check_vma=False
    )
```

profile of v0, /device:TPU:0, one launch (start us, length us, event | category | flops | bytes accessed | tf_op | source)
XLA Modules:
  0.0 1635.1 jit_solution(17745862805396485269)
XLA Ops:
  16.6 22.3 %all-gather = bf16[8,1,256]{2,1,0:T(2,128)(2,1)S(1)} all-gather(bf16[1,1,256]{2,1,0:T(2,128)(2,1)S(1)} %reshape.304), channel_id=1, replica_groups=mesh['dp'=8,'mp'=4] {'dp'}, dimensions={0}, use_global_device_ids=true | all-gather | bytes 4608 | tf_op jit(solution)/shard_map/all_gather | solution.py:114
  43.8 17.2 %all-reduce.7 = (bf16[128]{0:T(256)(128)(2,1)S(1)}, bf16[128]{0:T(256)(128)(2,1)S(1)}) all-reduce(bf16[128]{0:T(256)(128)(2,1)S(1)} %dynamic-update-slice, bf16[128]{0:T(256)(128)(2,1)S(1)} %dynamic-update-slice.1), channel_id=1, replica_groups=mesh['dp'=8,'mp'=4] {'dp'}, use_global_device_ids=true, to_apply=%add | all-reduce | flops 256 | bytes 1024
  63.7 4.0 multiply_reduce_fusion.7
  69.1 26.4 %all-gather.10.cloned.1.call-done = bf16[2048,256]{1,0:T(8,128)(2,1)} async-done(((bf16[256,256]{1,0:T(8,128)(2,1)}), bf16[2048,256]{1,0:T(8,128)(2,1)}) %all-gather.10.cloned.1.call-update) | async-done | bytes 1048592 | tf_op jit(solution)/shard_map/all_gather | solution.py:119
  95.5 4.0 convolution_convert_fusion.8
  99.5 46.8 %all-gather.14.cloned.1.call-done = bf16[2048,512]{1,0:T(8,128)(2,1)} async-done(((bf16[256,512]{1,0:T(8,128)(2,1)}), bf16[2048,512]{1,0:T(8,128)(2,1)}) %all-gather.14.cloned.1.call-update) | async-done | bytes 2097168 | tf_op jit(solution)/shard_map/all_gather | solution.py:117
  146.3 5.4 multiply_reduce_fusion.4
  164.0 34.4 %all-gather.16.cloned.1.call-done = bf16[512,2048]{1,0:T(8,128)(2,1)} async-done(((bf16[512,256]{1,0:T(8,128)(2,1)}), bf16[512,2048]{1,0:T(8,128)(2,1)}) %all-gather.16.cloned.1.call-update) | async-done | bytes 2097168 | tf_op jit(solution)/shard_map/all_gather | solution.py:120
  198.4 7.2 fusion.77
  212.0 17.4 %all-gather.1 = bf16[8,1,256]{2,1,0:T(2,128)(2,1)S(1)} all-gather(bf16[1,1,256]{2,1,0:T(2,128)(2,1)S(1)} %reshape.306), channel_id=1, replica_groups=mesh['dp'=8,'mp'=4] {'dp'}, dimensions={0}, use_global_device_ids=true | all-gather | bytes 4608 | tf_op jit(solution)/shard_map/all_gather | solution.py:132
  230.0 126.9 %all-reduce.14.cloned.1.call-done = f32[1024,2048]{1,0:T(8,128)} async-done(((f32[1024,2048]{1,0:T(8,128)}), f32[1024,2048]{1,0:T(8,128)}) %all-reduce.14.cloned.1.call-update) | async-done | bytes 8388624 | tf_op jit(solution)/shard_map/psum | solution.py:190
  356.8 5.7 multiply_reduce_fusion.1
  362.6 3.3 copy-done.2
  368.6 90.1 %all-gather.18.cloned.1.call-done = bf16[2048,1536]{1,0:T(8,128)(2,1)} async-done(((bf16[256,1536]{1,0:T(8,128)(2,1)}), bf16[2048,1536]{1,0:T(8,128)(2,1)}) %all-gather.18.cloned.1.call-update) | async-done | bytes 6291472 | tf_op jit(solution)/shard_map/all_gather | solution.py:133
  458.7 11.9 fusion.78
  470.6 88.1 %all-gather.20.cloned.1.call-done = bf16[2048,1536]{1,0:T(8,128)(2,1)} async-done(((bf16[256,1536]{1,0:T(8,128)(2,1)}), bf16[2048,1536]{1,0:T(8,128)(2,1)}) %all-gather.20.cloned.1.call-update) | async-done | bytes 6291472 | tf_op jit(solution)/shard_map/all_gather | solution.py:134
  558.7 11.7 fusion.79
  570.4 89.1 %all-gather.22.cloned.1.call-done = bf16[1536,2048]{1,0:T(8,128)(2,1)} async-done(((bf16[1536,256]{1,0:T(8,128)(2,1)}), bf16[1536,2048]{1,0:T(8,128)(2,1)}) %all-gather.22.cloned.1.call-update) | async-done | bytes 6291472 | tf_op jit(solution)/shard_map/all_gather | solution.py:135
  659.4 16.4 %multiply_convert_fusion.2 = (bf16[1024,1536]{1,0:T(8,128)(2,1)}, bf16[1024,1536]{1,0:T(8,128)(2,1)S(1)}, bf16[1024,1536]{1,0:T(8,128)(2,1)}) fusion(f32[1024,1536]{1,0:T(8,128)} %fusion.78, f32[1024,1536]{1,0:T(8,128)} %fusion.79, bf16[1024,2048]{1,0:T(8,128)(2,1)} %param.16, bf16[1536,2048]{1,0:T(8,128)(2,1)} %all-gather.22.cloned.1.call-done), kind=kOutput, calls=%fused_computation.43 | convolution fusion | flops 6466043904 | bytes 32505856 | tf_op jit(solution)/shard_map/dot_general | solution.py:65
  675.8 10.0 fusion.80
  685.8 10.2 add_convert_fusion.1
  696.2 11.3 convolution_convert_fusion.3
  707.5 72.4 %all-reduce.16.cloned.1.call-done = bf16[1024,2048]{1,0:T(8,128)(2,1)} async-done(((bf16[1024,2048]{1,0:T(8,128)(2,1)}), bf16[1024,2048]{1,0:T(8,128)(2,1)}) %all-reduce.16.cloned.1.call-update) | async-done | bytes 4194320 | tf_op jit(solution)/shard_map/psum | solution.py:216
  779.9 6.0 fusion.5
  787.0 5.0 fusion.4
  800.2 5.0 fusion.7
  805.2 5.1 fusion.9
  828.8 4.9 convolution_convert_fusion.6
  833.9 5.1 fusion.33
  843.4 3.3 add_convert_fusion
  846.8 4.9 convolution_convert_fusion.7
  851.8 6.5 convolution_convert_fusion.5
  858.6 7.1 convolution_convert_fusion.4
  865.8 11.5 convolution_convert_fusion.2
  879.2 11.0 convolution_convert_fusion.1
  892.1 10.9 convolution_convert_fusion
  906.1 146.2 %all-reduce.18.cloned.1.call-done = (bf16[1024,2048]{1,0:T(8,128)(2,1)}, bf16[1024,2048]{1,0:T(8,128)(2,1)}) async-done(((bf16[1024,2048]{1,0:T(8,128)(2,1)}, bf16[1024,2048]{1,0:T(8,128)(2,1)}), (bf16[1024,2048]{1,0:T(8,128)(2,1)}, bf16[1024,2048]{1,0:T(8,128)(2,1)})) %all-reduce.18.cloned.1.call-update) | async-done | bytes 8388624 | tf_op jit(solution)/shard_map/psum | solution.py:201
  1052.2 6.5 multiply_reduce_fusion
  1058.8 22.0 %all-reduce.6 = (bf16[2048]{0:T(1024)(128)(2,1)S(1)}, bf16[128]{0:T(256)(128)(2,1)S(1)}, bf16[128]{0:T(256)(128)(2,1)S(1)}, bf16[2048]{0:T(1024)(128)(2,1)S(1)}) all-reduce(bf16[2048]{0:T(1024)(128)(2,1)S(1)} %get-tuple-element.84, bf16[128]{0:T(256)(128)(2,1)S(1)} %reduce_sum.170, ...), channel_id=2, replica_groups=mesh['dp'=8,'mp'=4] {'dp'}, use_global_device_ids=true, to_apply=%region_21.22.clone | all-reduce | flops 4352 | bytes 17408
  1081.0 38.8 %reduce-scatter.10.cloned.1.call-done = bf16[256,256]{1,0:T(8,128)(2,1)} async-done(((bf16[2048,256]{1,0:T(8,128)(2,1)}), bf16[256,256]{1,0:T(8,128)(2,1)}) %reduce-scatter.10.cloned.1.call-update) | async-done | bytes 131088 | tf_op jit(solution)/shard_map/reduce_scatter | solution.py:315
  1121.4 5.6 all-reduce.8
  1127.0 6.7 convert_element_type.272
  1134.7 56.6 %reduce-scatter.8.cloned.1.call-done = bf16[256,512]{1,0:T(8,128)(2,1)} async-done(((bf16[2048,512]{1,0:T(8,128)(2,1)}), bf16[256,512]{1,0:T(8,128)(2,1)}) %reduce-scatter.8.cloned.1.call-update) | async-done | bytes 262160 | tf_op jit(solution)/shard_map/reduce_scatter | solution.py:312
  1193.1 69.3 %reduce-scatter.14.cloned.1.call-done = bf16[512,256]{1,0:T(8,128)(2,1)} async-done(((bf16[512,2048]{1,0:T(8,128)(2,1)}), bf16[512,256]{1,0:T(8,128)(2,1)}) %reduce-scatter.14.cloned.1.call-update) | async-done | bytes 262160 | tf_op jit(solution)/shard_map/reduce_scatter | solution.py:321
  1267.3 6.0 multiply_add_fusion
  1273.3 110.0 %reduce-scatter.16.cloned.1.call-done = bf16[256,1536]{1,0:T(8,128)(2,1)} async-done(((bf16[2048,1536]{1,0:T(8,128)(2,1)}), bf16[256,1536]{1,0:T(8,128)(2,1)}) %reduce-scatter.16.cloned.1.call-update) | async-done | bytes 786448 | tf_op jit(solution)/shard_map/reduce_scatter | solution.py:329
  1385.7 118.5 %reduce-scatter.18.cloned.1.call-done = bf16[256,1536]{1,0:T(8,128)(2,1)} async-done(((bf16[2048,1536]{1,0:T(8,128)(2,1)}), bf16[256,1536]{1,0:T(8,128)(2,1)}) %reduce-scatter.18.cloned.1.call-update) | async-done | bytes 786448 | tf_op jit(solution)/shard_map/reduce_scatter | solution.py:332
  1506.7 119.0 %reduce-scatter.20.cloned.1.call-done = bf16[1536,256]{1,0:T(8,128)(2,1)} async-done(((bf16[1536,2048]{1,0:T(8,128)(2,1)}), bf16[1536,256]{1,0:T(8,128)(2,1)}) %reduce-scatter.20.cloned.1.call-update) | async-done | bytes 786448 | tf_op jit(solution)/shard_map/reduce_scatter | solution.py:335
  (257 shorter events, 94.1 us)
Async XLA Ops:
  7.2 34.9 %copy-start.45 = (u32[32]{0:T(128)S(1)}, u32[32]{0:T(128)}, u32[]{:S(2)}) copy-start(u32[32]{0:T(128)} %constant.106) | copy-start | bytes 388
  7.2 34.8 %copy-start.50 = (f32[16]{0:T(128)S(1)}, f32[16]{0:T(128)}, u32[]{:S(2)}) copy-start(f32[16]{0:T(128)} %param.19) | copy-start | bytes 196
  7.2 34.8 %copy-start.51 = (f32[16]{0:T(128)S(1)}, f32[16]{0:T(128)}, u32[]{:S(2)}) copy-start(f32[16]{0:T(128)} %param.18) | copy-start | bytes 196
  7.2 56.4 %all-gather.12.cloned.1.call-start = ((), (), s32[]{:S(2)}) async-start(), calls=%async_computation.8 | async-start | bytes 1179648 | tf_op jit(solution)/shard_map/all_gather | solution.py:118
  8.9 86.6 %all-gather.10.cloned.1.call-start = ((), (), s32[]{:S(2)}) async-start(), calls=%async_computation.7 | async-start | bytes 1179648 | tf_op jit(solution)/shard_map/all_gather | solution.py:119
  10.6 52.3 %copy-start.39 = (s32[1,1024]{1,0:T(1,128)S(1)}, s32[1,1024]{1,0:T(1,128)}, u32[]{:S(2)}) copy-start(s32[1,1024]{1,0:T(1,128)} %param.15) | copy-start | bytes 12292
  10.6 135.7 %all-gather.14.cloned.1.call-start = ((), (), s32[]{:S(2)}) async-start(), calls=%async_computation.9 | async-start | bytes 2359296 | tf_op jit(solution)/shard_map/all_gather | solution.py:117
  12.5 185.9 %all-gather.16.cloned.1.call-start = ((), (), s32[]{:S(2)}) async-start(), calls=%async_computation.10 | async-start | bytes 2359296 | tf_op jit(solution)/shard_map/all_gather | solution.py:120
  14.3 342.5 %all-reduce.14.cloned.1.call-start = ((), (), s32[]{:S(2)}) async-start(), calls=%async_computation.11 | async-start | bytes 16777216 | tf_op jit(solution)/shard_map/psum | solution.py:190
  38.9 107.4 %copy-start.37 = (f32[8,1,256]{2,1,0:T(1,128)}, f32[8,1,256]{2,1,0:T(1,128)S(1)}, u32[]{:S(2)}) copy-start(f32[8,1,256]{2,1,0:T(1,128)S(1)} %convert_element_type.295) | copy-start | bytes 24580
  42.0 104.3 %copy-start.40 = (f32[1024]{0:T(1024)}, f32[1024]{0:T(1024)S(1)}, u32[]{:S(2)}) copy-start(f32[1024]{0:T(1024)S(1)} %add_rsqrt_fusion.3) | copy-start | bytes 12292
  61.0 7.0 copy-start.43
  62.9 89.5 %copy-start.7 = (f32[1024,128]{0,1:T(8,128)}, f32[1024,128]{0,1:T(8,128)S(1)}, u32[]{:S(2)}) copy-start(f32[1024,128]{0,1:T(8,128)S(1)} %pad_maximum_fusion.4) | copy-start | bytes 1572868
  62.9 89.4 %copy-start.9 = (f32[1024,128]{0,1:T(8,128)}, f32[1024,128]{0,1:T(8,128)S(1)}, u32[]{:S(2)}) copy-start(f32[1024,128]{0,1:T(8,128)S(1)} %pad_maximum_fusion.5) | copy-start | bytes 1572868
  69.1 88.1 %copy-start.16 = (bf16[1024,2,128,1]{0,2,3,1:T(8,128)(2,1)}, bf16[1024,2,128,1]{0,2,3,1:T(8,128)(2,1)S(1)}, u32[]{:S(2)}) copy-start(bf16[1024,2,128,1]{0,2,3,1:T(8,128)(2,1)S(1)} %fusion.64) | copy-start | bytes 1572868
  153.9 3.3 copy-start.20
  155.6 4.5 copy-start
  163.9 41.7 %copy-start.33 = (bf16[1024,2,2,128]{0,3,2,1:T(8,128)(2,1)}, bf16[1024,2,2,128]{0,3,2,1:T(8,128)(2,1)S(1)}, u32[]{:S(2)}) copy-start(bf16[1024,2,2,128]{0,3,2,1:T(8,128)(2,1)S(1)} %pad_maximum_fusion.3) | copy-start | bytes 3145732
  205.6 6.3 copy-start.49
  205.6 253.0 %all-gather.18.cloned.1.call-start = ((), (), s32[]{:S(2)}) async-start(), calls=%async_computation.12 | async-start | bytes 7077888 | tf_op jit(solution)/shard_map/all_gather | solution.py:133
  208.0 350.7 %all-gather.20.cloned.1.call-start = ((), (), s32[]{:S(2)}) async-start(), calls=%async_computation.13 | async-start | bytes 7077888 | tf_op jit(solution)/shard_map/all_gather | solution.py:134
  210.8 448.6 %all-gather.22.cloned.1.call-start = ((), (), s32[]{:S(2)}) async-start(), calls=%async_computation.14 | async-start | bytes 7077888 | tf_op jit(solution)/shard_map/all_gather | solution.py:135
  211.9 568.0 %all-reduce.16.cloned.1.call-start = ((), (), s32[]{:S(2)}) async-start(), calls=%async_computation.15 | async-start | bytes 8388608 | tf_op jit(solution)/shard_map/psum | solution.py:216
  675.8 10.0 copy-start.52
  675.8 10.0 copy-start.46
  696.1 208.3 %reduce-scatter.12.cloned.1.call-start = ((), (), s32[]{:S(2)}) async-start(), calls=%async_computation.18 | async-start | bytes 1179648 | tf_op jit(solution)/shard_map/reduce_scatter | solution.py:318
  779.9 6.0 copy-start.12
  779.9 7.1 copy-start.24
  779.9 15.5 slice-start
  787.0 5.0 copy-start.48
  787.0 8.5 slice-start.1
  792.0 3.3 copy-start.15
  795.5 4.4 slice-start.2
  805.2 5.1 copy-start.21
  814.0 12.5 copy-start.13
  820.4 6.2 copy-start.14
  828.7 5.2 copy-start.42
  833.7 218.6 %all-reduce.18.cloned.1.call-start = ((), (), s32[]{:S(2)}) async-start(), calls=%async_computation.23 | async-start | bytes 16777216 | tf_op jit(solution)/shard_map/psum | solution.py:201
  833.9 5.1 copy-start.22
  833.9 5.4 copy-start.29
  846.7 5.0 copy-start.32
  846.7 273.0 %reduce-scatter.10.cloned.1.call-start = ((), (), s32[]{:S(2)}) async-start(), calls=%async_computation.17 | async-start | bytes 1179648 | tf_op jit(solution)/shard_map/reduce_scatter | solution.py:315
  851.7 6.9 copy-start.34
  851.7 339.5 %reduce-scatter.8.cloned.1.call-start = ((), (), s32[]{:S(2)}) async-start(), calls=%async_computation.16 | async-start | bytes 2359296 | tf_op jit(solution)/shard_map/reduce_scatter | solution.py:312
  858.3 404.0 %reduce-scatter.14.cloned.1.call-start = ((), (), s32[]{:S(2)}) async-start(), calls=%async_computation.19 | async-start | bytes 2359296 | tf_op jit(solution)/shard_map/reduce_scatter | solution.py:321
  865.7 517.5 %reduce-scatter.16.cloned.1.call-start = ((), (), s32[]{:S(2)}) async-start(), calls=%async_computation.20 | async-start | bytes 7077888 | tf_op jit(solution)/shard_map/reduce_scatter | solution.py:329
  877.3 627.0 %reduce-scatter.18.cloned.1.call-start = ((), (), s32[]{:S(2)}) async-start(), calls=%async_computation.21 | async-start | bytes 7077888 | tf_op jit(solution)/shard_map/reduce_scatter | solution.py:332
  890.2 735.5 %reduce-scatter.20.cloned.1.call-start = ((), (), s32[]{:S(2)}) async-start(), calls=%async_computation.22 | async-start | bytes 7077888 | tf_op jit(solution)/shard_map/reduce_scatter | solution.py:335
  (28 other events, 52.7 us)
Sparse Core Ops, SparseCore 0:
  10.7 42.9 all-gather.11
  56.4 39.0 all-gather.9
  98.2 48.0 all-gather.13
  148.8 49.5 all-gather.15
  205.8 151.0 all-reduce.13
  359.5 99.1 all-gather.17
  461.4 97.1 all-gather.19
  561.3 98.1 all-gather.21
  696.2 83.6 all-reduce.15
  833.8 63.5 reduce-scatter.11
  900.0 152.2 all-reduce.17
  1056.1 63.6 reduce-scatter.9
  1124.3 66.9 reduce-scatter.7
  1195.0 67.2 reduce-scatter.13
  1266.2 117.0 reduce-scatter.15
  1387.1 117.0 reduce-scatter.17
  1508.2 117.5 reduce-scatter.19
where the time goes:
time: 1650 us; the launch traced here: 1640 us
  waiting for transfers between devices  1230 us (75%)
  matrix products  182 us (11%)
  other arithmetic  98.9 us (6%)
  blocking collectives  84.5 us (5%)
  local copies, waits for them, and re-layouts  17.7 us (1%)
  between operations  17.4 us (1%)
    psum x1, waiting for transfers between devices, on_device(): lax.psum(mlp_part.astype(jnp.bfloat16), 'mp').astype(jnp.float32)  146 us
    psum x1, waiting for transfers between devices, on_device(): hidden = inputs + lax.psum(attn_part, 'mp')  127 us
    reduce_scatter x1, waiting for transfers between devices, on_device(): lax.psum_scatter(down_grad.astype(jnp.bfloat16), 'dp', scatter_dimension=...  119 us
    reduce_scatter x1, waiting for transfers between devices, on_device(): lax.psum_scatter(up_grad.astype(jnp.bfloat16), 'dp', scatter_dimension=0,...  119 us
    reduce_scatter x1, waiting for transfers between devices, on_device(): lax.psum_scatter(gate_grad.astype(jnp.bfloat16), 'dp', scatter_dimension=...  110 us
    all_gather x1, waiting for transfers between devices, on_device(): lax.all_gather(gate_weight.astype(jnp.bfloat16), 'dp', axis=0, tiled=True)  90.1 us
    all_gather x1, waiting for transfers between devices, on_device(): lax.all_gather(down_weight.astype(jnp.bfloat16), 'dp', axis=1, tiled=True)  89.1 us
    all_gather x1, waiting for transfers between devices, on_device(): lax.all_gather(up_weight.astype(jnp.bfloat16), 'dp', axis=0, tiled=True)  88.1 us
  transfers between devices with their start and end apart: 17, of which 15 were waited for; matrix products, arithmetic and copies ran while one was open for 11% of the time, Pallas kernels for 0%

commit v1 on v0

--- a/solution.py
+++ b/solution.py
@@ -1,3 +1,4 @@
+import functools
 import jax
 import jax.numpy as jnp
 from jax import lax
@@ -8,6 +9,30 @@
 HEAD_WIDTH = 128
 EPSILON = 1e-06
 MASKED = -1e30
+
+
+def _settle_circles(s0, row_dim):
+    n_blocks = jax.lax.axis_size("dp")
+    moved = range(n_blocks)
+    local_out = map(lambda it: (it, (it + 1) % n_blocks), moved)
+    buffers = list(local_out)
+    t1 = range(n_blocks)
+    after = map(lambda it: (it, (it - 1) % n_blocks), t1)
+    pieces_in = list(after)
+    value_now, block_now = ([s0], [s0])
+    for _ in range(n_blocks // 2):
+        x_new = jax.lax.ppermute(value_now[-1], axis_name="dp", perm=buffers)
+        value_now.append(x_new)
+    for _ in range((n_blocks - 1) // 2):
+        seen_now = jax.lax.ppermute(block_now[-1], axis_name="dp", perm=pieces_in)
+        block_now.append(seen_now)
+    z = jnp.concatenate([*value_now[::-1], *block_now[1:]], axis=row_dim)
+    f_now = jax.lax.axis_index("dp")
+    z1 = jnp.roll(z, (f_now - n_blocks // 2) * s0.shape[row_dim], axis=row_dim)
+    return z1
+
+
+link_the_edge = functools.partial(_settle_circles, row_dim=1)
 
 
 def doc_positions(documents):
@@ -132,7 +157,7 @@
         lax.all_gather(mlp_gain.astype(jnp.bfloat16), "dp", axis=0, tiled=True),
         lax.all_gather(gate_weight.astype(jnp.bfloat16), "dp", axis=0, tiled=True),
         lax.all_gather(up_weight.astype(jnp.bfloat16), "dp", axis=0, tiled=True),
-        lax.all_gather(down_weight.astype(jnp.bfloat16), "dp", axis=1, tiled=True),
+        link_the_edge(down_weight.astype(jnp.bfloat16)),
     )
     gain_two = mlp_parts[0].astype(jnp.float32)
     gate_mat, up_mat, down_mat = (mlp_parts[1], mlp_parts[2], mlp_parts[3])

time: 1650 us -> 1550 us (0.939)
  waiting for transfers between devices: 1230 us -> 1070 us
  starting transfers between devices: 1.34 us -> 30.2 us
  local copies, waits for them, and re-layouts: 17.7 us -> 42.3 us
    psum x1, waiting for transfers between devices: 127 us -> 0.01 us  [on_device(): hidden = inputs + lax.psum(attn_part, 'mp')]
    all_gather x1 -> x0, waiting for transfers between devices: 89.1 us -> none  [on_device(): lax.all_gather(down_weight.astype(jnp.bfloat16), 'dp', axis=1, tiled=True)]
    ppermute x0 -> x7, waiting for transfers between devices: none -> 64.7 us  [the longest x4 59.7 us: _settle_circles(): x_new = jax.lax.ppermute(value_now[-1], axis_name='dp', perm=buffers)]
    reduce_scatter x1, waiting for transfers between devices: 0.01 us -> 38.9 us  [on_device(): lax.psum_scatter(value_grad.astype(jnp.bfloat16), 'dp', scatter_dimension...]
    reduce_scatter x1, waiting for transfers between devices: 38.8 us -> 0.02 us  [on_device(): lax.psum_scatter(key_grad.astype(jnp.bfloat16), 'dp', scatter_dimension=0...]
    ppermute x0 -> x7, starting transfers between devices: none -> 28.9 us  [the longest x3 22.3 us: _settle_circles(): seen_now = jax.lax.ppermute(block_now[-1], axis_name='dp', perm=pieces_in)]
    unnamed x127 -> x176, local copies, waits for them, and re-layouts: 15.9 us -> 40.1 us
  transfers between devices with their start and end apart: 17 -> 23, of which waited for: 15 -> 17; matrix products, arithmetic and copies ran while one was open for 11% -> 13% of each run, Pallas kernels for 0% -> 0%
where the time goes in v1:
time: 1550 us; the launch traced here: 1540 us
  waiting for transfers between devices  1070 us (69%)
  matrix products  182 us (12%)
  blocking collectives  98.4 us (6%)
  other arithmetic  96.3 us (6%)
  local copies, waits for them, and re-layouts  42.3 us (3%)
  starting transfers between devices  30.2 us (2%)
  between operations  17.6 us (1%)
    psum x1, waiting for transfers between devices, on_device(): lax.psum(mlp_part.astype(jnp.bfloat16), 'mp').astype(jnp.float32)  137 us
    reduce_scatter x1, waiting for transfers between devices, on_device(): lax.psum_scatter(down_grad.astype(jnp.bfloat16), 'dp', scatter_dimension=...  119 us
    reduce_scatter x1, waiting for transfers between devices, on_device(): lax.psum_scatter(up_grad.astype(jnp.bfloat16), 'dp', scatter_dimension=0,...  119 us
    reduce_scatter x1, waiting for transfers between devices, on_device(): lax.psum_scatter(gate_grad.astype(jnp.bfloat16), 'dp', scatter_dimension=...  110 us
    all_gather x1, waiting for transfers between devices, on_device(): lax.all_gather(up_weight.astype(jnp.bfloat16), 'dp', axis=0, tiled=True)  88.1 us
    all_gather x1, waiting for transfers between devices, on_device(): lax.all_gather(gate_weight.astype(jnp.bfloat16), 'dp', axis=0, tiled=True)  87.3 us
    psum x1, waiting for transfers between devices, on_device(): lax.psum(normed_two_part.astype(jnp.bfloat16), 'mp').astype(jnp.float32)  72.6 us
    reduce_scatter x1, waiting for transfers between devices, on_device(): lax.psum_scatter(output_grad.astype(jnp.bfloat16), 'dp', scatter_dimensio...  69.5 us
  transfers between devices with their start and end apart: 23, of which 17 were waited for; matrix products, arithmetic and copies ran while one was open for 13% of the time, Pallas kernels for 0%

profile of v1, /device:TPU:0, one launch (start us, length us, event | category | flops | bytes accessed | tf_op | source)
XLA Modules:
  0.0 1538.2 jit_solution(12975955192849788757)
XLA Ops:
  16.6 22.3 %all-gather = bf16[8,1,256]{2,1,0:T(2,128)(2,1)S(1)} all-gather(bf16[1,1,256]{2,1,0:T(2,128)(2,1)S(1)} %reshape.304), channel_id=1, replica_groups=mesh['dp'=8,'mp'=4] {'dp'}, dimensions={0}, use_global_device_ids=true | all-gather | bytes 4608 | tf_op jit(solution)/shard_map/all_gather | solution.py:139
  43.8 17.2 %all-reduce.7 = (bf16[128]{0:T(256)(128)(2,1)S(1)}, bf16[128]{0:T(256)(128)(2,1)S(1)}) all-reduce(bf16[128]{0:T(256)(128)(2,1)S(1)} %dynamic-update-slice, bf16[128]{0:T(256)(128)(2,1)S(1)} %dynamic-update-slice.1), channel_id=1, replica_groups=mesh['dp'=8,'mp'=4] {'dp'}, use_global_device_ids=true, to_apply=%add | all-reduce | flops 256 | bytes 1024
  63.7 4.0 multiply_reduce_fusion.7
  69.1 26.5 %all-gather.9.cloned.1.call-done = bf16[2048,256]{1,0:T(8,128)(2,1)} async-done(((bf16[256,256]{1,0:T(8,128)(2,1)}), bf16[2048,256]{1,0:T(8,128)(2,1)}) %all-gather.9.cloned.1.call-update) | async-done | bytes 1048592 | tf_op jit(solution)/shard_map/all_gather | solution.py:144
  99.6 46.8 %all-gather.13.cloned.1.call-done = bf16[2048,512]{1,0:T(8,128)(2,1)} async-done(((bf16[256,512]{1,0:T(8,128)(2,1)}), bf16[2048,512]{1,0:T(8,128)(2,1)}) %all-gather.13.cloned.1.call-update) | async-done | bytes 2097168 | tf_op jit(solution)/shard_map/all_gather | solution.py:142
  146.4 5.4 multiply_reduce_fusion.4
  163.5 35.0 %all-gather.15.cloned.1.call-done = bf16[512,2048]{1,0:T(8,128)(2,1)} async-done(((bf16[512,256]{1,0:T(8,128)(2,1)}), bf16[512,2048]{1,0:T(8,128)(2,1)}) %all-gather.15.cloned.1.call-update) | async-done | bytes 2097168 | tf_op jit(solution)/shard_map/all_gather | solution.py:145
  198.5 7.3 fusion.90
  212.3 17.4 %collective-permute-done = bf16[1536,256]{1,0:T(8,128)(2,1)S(1)} collective-permute-done((bf16[1536,256]{1,0:T(8,128)(2,1)S(1)}, bf16[1536,256]{1,0:T(8,128)(2,1)S(1)}, u32[]{:S(2)}, u32[]{:S(2)}) %collective-permute-start) | collective-permute-done | bytes 786464 | tf_op jit(solution)/shard_map/ppermute | solution.py:24
  229.7 4.7 collective-permute-start.4
  234.4 28.0 %collective-permute-done.1 = bf16[1536,256]{1,0:T(8,128)(2,1)S(1)} collective-permute-done((bf16[1536,256]{1,0:T(8,128)(2,1)S(1)}, bf16[1536,256]{1,0:T(8,128)(2,1)S(1)}, u32[]{:S(2)}, u32[]{:S(2)}) %collective-permute-start.1) | collective-permute-done | bytes 786464 | tf_op jit(solution)/shard_map/ppermute | solution.py:24
  264.9 17.5 %collective-permute-start.5 = (bf16[1536,256]{1,0:T(8,128)(2,1)S(1)}, bf16[1536,256]{1,0:T(8,128)(2,1)}, u32[]{:S(2)}, u32[]{:S(2)}) collective-permute-start(bf16[1536,256]{1,0:T(8,128)(2,1)S(1)} %collective-permute-done.4), channel_id=1, source_target_pairs={{0,28},{4,0},{8,4},{12,8},{16,12},{20,16},{24,20},{28,24},{1,29},{... | collective-permute-start | bytes 2359304 | tf_op jit(solution)/shard_map/ppermute | solution.py:27
  282.4 14.3 collective-permute-done.2
  299.4 31.2 %all-gather.1 = bf16[8,1,256]{2,1,0:T(2,128)(2,1)S(1)} all-gather(bf16[1,1,256]{2,1,0:T(2,128)(2,1)S(1)} %reshape.306), channel_id=1, replica_groups=mesh['dp'=8,'mp'=4] {'dp'}, dimensions={0}, use_global_device_ids=true | all-gather | bytes 4608 | tf_op jit(solution)/shard_map/all_gather | solution.py:157
  342.4 4.9 collective-permute-done.6
  359.6 5.7 multiply_reduce_fusion.1
  371.5 87.3 %all-gather.17.cloned.1.call-done = bf16[2048,1536]{1,0:T(8,128)(2,1)} async-done(((bf16[256,1536]{1,0:T(8,128)(2,1)}), bf16[2048,1536]{1,0:T(8,128)(2,1)}) %all-gather.17.cloned.1.call-update) | async-done | bytes 6291472 | tf_op jit(solution)/shard_map/all_gather | solution.py:158
  458.8 11.9 fusion.91
  470.7 88.1 %all-gather.19.cloned.1.call-done = bf16[2048,1536]{1,0:T(8,128)(2,1)} async-done(((bf16[256,1536]{1,0:T(8,128)(2,1)}), bf16[2048,1536]{1,0:T(8,128)(2,1)}) %all-gather.19.cloned.1.call-update) | async-done | bytes 6291472 | tf_op jit(solution)/shard_map/all_gather | solution.py:159
  558.8 11.9 fusion.92
  570.7 16.2 %fusion.20 = (bf16[1024,1536]{1,0:T(8,128)(2,1)}, bf16[1024,1536]{1,0:T(8,128)(2,1)}, bf16[1024,1536]{1,0:T(8,128)(2,1)}) fusion(f32[1024,1536]{1,0:T(8,128)} %fusion.91, f32[1024,1536]{1,0:T(8,128)} %fusion.92, bf16[1024,2048]{1,0:T(8,128)(2,1)S(1)} %copy-done.30, bf16[1536,4096]{1,0:T(8,128)(2,1)} %constant_dynamic-update-slice_fusion, s32[]{:T(128)S(6)} %select_n.52), kind=kOutput, calls=%fused_computation.48 | convolution fusion | flops 6466043904 | bytes 32505860 | tf_op jit(solution)/shard_map/dot_general | solution.py:90
  586.9 10.6 fusion.93
  597.4 10.8 add_convert_fusion.1
  608.4 11.1 fusion.34
  619.4 72.6 %all-reduce.16.cloned.1.call-done = bf16[1024,2048]{1,0:T(8,128)(2,1)} async-done(((bf16[1024,2048]{1,0:T(8,128)(2,1)}), bf16[1024,2048]{1,0:T(8,128)(2,1)}) %all-reduce.16.cloned.1.call-update) | async-done | bytes 4194320 | tf_op jit(solution)/shard_map/psum | solution.py:241
  692.1 6.0 fusion.5
  699.2 5.0 fusion.4
  727.1 4.4 broadcast_multiply_fusion
  737.0 4.7 fusion.44
  742.7 5.7 fusion.94
  758.6 4.9 convolution_convert_fusion.5
  763.8 6.5 convolution_convert_fusion.4
  770.4 7.1 convolution_convert_fusion.3
  777.6 11.6 convolution_convert_fusion.2
  791.0 11.0 convolution_convert_fusion.1
  803.9 10.8 convolution_convert_fusion
  817.8 137.3 %all-reduce.18.cloned.1.call-done = (bf16[1024,2048]{1,0:T(8,128)(2,1)}, bf16[1024,2048]{1,0:T(8,128)(2,1)}) async-done(((bf16[1024,2048]{1,0:T(8,128)(2,1)}, bf16[1024,2048]{1,0:T(8,128)(2,1)}), (bf16[1024,2048]{1,0:T(8,128)(2,1)}, bf16[1024,2048]{1,0:T(8,128)(2,1)})) %all-reduce.18.cloned.1.call-update) | async-done | bytes 8388624 | tf_op jit(solution)/shard_map/psum | solution.py:226
  955.1 6.5 multiply_reduce_fusion
  961.6 22.2 %all-reduce.6 = (bf16[2048]{0:T(1024)(128)(2,1)S(1)}, bf16[128]{0:T(256)(128)(2,1)S(1)}, bf16[128]{0:T(256)(128)(2,1)S(1)}, bf16[2048]{0:T(1024)(128)(2,1)S(1)}) all-reduce(bf16[2048]{0:T(1024)(128)(2,1)S(1)} %get-tuple-element.84, bf16[128]{0:T(256)(128)(2,1)S(1)} %reduce_sum.170, ...), channel_id=2, replica_groups=mesh['dp'=8,'mp'=4] {'dp'}, use_global_device_ids=true, to_apply=%region_21.22.clone | all-reduce | flops 4352 | bytes 17408
  983.9 38.9 %reduce-scatter.12.cloned.1.call-done = bf16[256,256]{1,0:T(8,128)(2,1)} async-done(((bf16[2048,256]{1,0:T(8,128)(2,1)}), bf16[256,256]{1,0:T(8,128)(2,1)}) %reduce-scatter.12.cloned.1.call-update) | async-done | bytes 131088 | tf_op jit(solution)/shard_map/reduce_scatter | solution.py:343
  1024.5 5.6 all-reduce.8
  1030.1 6.6 convert_element_type.272
  1037.7 56.6 %reduce-scatter.8.cloned.1.call-done = bf16[256,512]{1,0:T(8,128)(2,1)} async-done(((bf16[2048,512]{1,0:T(8,128)(2,1)}), bf16[256,512]{1,0:T(8,128)(2,1)}) %reduce-scatter.8.cloned.1.call-update) | async-done | bytes 262160 | tf_op jit(solution)/shard_map/reduce_scatter | solution.py:337
  1096.1 69.5 %reduce-scatter.14.cloned.1.call-done = bf16[512,256]{1,0:T(8,128)(2,1)} async-done(((bf16[512,2048]{1,0:T(8,128)(2,1)}), bf16[512,256]{1,0:T(8,128)(2,1)}) %reduce-scatter.14.cloned.1.call-update) | async-done | bytes 262160 | tf_op jit(solution)/shard_map/reduce_scatter | solution.py:346
  1170.6 6.0 multiply_add_fusion
  1176.6 109.8 %reduce-scatter.16.cloned.1.call-done = bf16[256,1536]{1,0:T(8,128)(2,1)} async-done(((bf16[2048,1536]{1,0:T(8,128)(2,1)}), bf16[256,1536]{1,0:T(8,128)(2,1)}) %reduce-scatter.16.cloned.1.call-update) | async-done | bytes 786448 | tf_op jit(solution)/shard_map/reduce_scatter | solution.py:354
  1288.9 118.6 %reduce-scatter.18.cloned.1.call-done = bf16[256,1536]{1,0:T(8,128)(2,1)} async-done(((bf16[2048,1536]{1,0:T(8,128)(2,1)}), bf16[256,1536]{1,0:T(8,128)(2,1)}) %reduce-scatter.18.cloned.1.call-update) | async-done | bytes 786448 | tf_op jit(solution)/shard_map/reduce_scatter | solution.py:357
  1409.9 119.0 %reduce-scatter.20.cloned.1.call-done = bf16[1536,256]{1,0:T(8,128)(2,1)} async-done(((bf16[1536,2048]{1,0:T(8,128)(2,1)}), bf16[1536,256]{1,0:T(8,128)(2,1)}) %reduce-scatter.20.cloned.1.call-update) | async-done | bytes 786448 | tf_op jit(solution)/shard_map/reduce_scatter | solution.py:360
  (324 shorter events, 137.8 us)
Async XLA Ops:
  7.2 34.9 %copy-start.55 = (u32[32]{0:T(128)S(1)}, u32[32]{0:T(128)}, u32[]{:S(2)}) copy-start(u32[32]{0:T(128)} %constant.135) | copy-start | bytes 388
  7.2 55.8 %copy-start.50 = (s32[1,1024]{1,0:T(1,128)S(1)}, s32[1,1024]{1,0:T(1,128)}, u32[]{:S(2)}) copy-start(s32[1,1024]{1,0:T(1,128)} %param.15) | copy-start | bytes 12292
  7.2 34.8 %copy-start.60 = (f32[16]{0:T(128)S(1)}, f32[16]{0:T(128)}, u32[]{:S(2)}) copy-start(f32[16]{0:T(128)} %param.19) | copy-start | bytes 196
  7.2 34.8 %copy-start.61 = (f32[16]{0:T(128)S(1)}, f32[16]{0:T(128)}, u32[]{:S(2)}) copy-start(f32[16]{0:T(128)} %param.18) | copy-start | bytes 196
  7.2 56.5 %all-gather.11.cloned.1.call-start = ((), (), s32[]{:S(2)}) async-start(), calls=%async_computation.8 | async-start | bytes 1179648 | tf_op jit(solution)/shard_map/all_gather | solution.py:143
  8.9 86.7 %all-gather.9.cloned.1.call-start = ((), (), s32[]{:S(2)}) async-start(), calls=%async_computation.7 | async-start | bytes 1179648 | tf_op jit(solution)/shard_map/all_gather | solution.py:144
  10.6 135.8 %all-gather.13.cloned.1.call-start = ((), (), s32[]{:S(2)}) async-start(), calls=%async_computation.9 | async-start | bytes 2359296 | tf_op jit(solution)/shard_map/all_gather | solution.py:142
  12.5 186.0 %all-gather.15.cloned.1.call-start = ((), (), s32[]{:S(2)}) async-start(), calls=%async_computation.10 | async-start | bytes 2359296 | tf_op jit(solution)/shard_map/all_gather | solution.py:145
  14.3 345.3 %all-reduce.14.cloned.1.call-start = ((), (), s32[]{:S(2)}) async-start(), calls=%async_computation.11 | async-start | bytes 16777216 | tf_op jit(solution)/shard_map/psum | solution.py:215
  38.9 107.5 %copy-start.48 = (f32[8,1,256]{2,1,0:T(1,128)}, f32[8,1,256]{2,1,0:T(1,128)S(1)}, u32[]{:S(2)}) copy-start(f32[8,1,256]{2,1,0:T(1,128)S(1)} %convert_element_type.295) | copy-start | bytes 24580
  42.0 104.4 %copy-start.51 = (f32[1024]{0:T(1024)}, f32[1024]{0:T(1024)S(1)}, u32[]{:S(2)}) copy-start(f32[1024]{0:T(1024)S(1)} %add_rsqrt_fusion.3) | copy-start | bytes 12292
  62.9 89.5 %copy-start.13 = (f32[1024,128]{0,1:T(8,128)}, f32[1024,128]{0,1:T(8,128)S(1)}, u32[]{:S(2)}) copy-start(f32[1024,128]{0,1:T(8,128)S(1)} %pad_maximum_fusion.5) | copy-start | bytes 1572868
  63.0 89.4 %copy-start.9 = (f32[1024,128]{0,1:T(8,128)}, f32[1024,128]{0,1:T(8,128)S(1)}, u32[]{:S(2)}) copy-start(f32[1024,128]{0,1:T(8,128)S(1)} %pad_maximum_fusion.4) | copy-start | bytes 1572868
  69.1 87.5 %copy-start.21 = (bf16[1024,2,128,1]{0,2,3,1:T(8,128)(2,1)}, bf16[1024,2,128,1]{0,2,3,1:T(8,128)(2,1)S(1)}, u32[]{:S(2)}) copy-start(bf16[1024,2,128,1]{0,2,3,1:T(8,128)(2,1)S(1)} %fusion.75) | copy-start | bytes 1572868
  99.6 61.6 %copy-start.36 = (bf16[1024,256]{0,1:T(8,128)(2,1)}, bf16[1024,256]{0,1:T(8,128)(2,1)S(1)}, u32[]{:S(2)}) copy-start(bf16[1024,256]{0,1:T(8,128)(2,1)S(1)} %convolution_convert_fusion.7) | copy-start | bytes 1572868
  163.4 35.0 %copy-start.43 = (bf16[1024,2,2,128]{0,3,2,1:T(8,128)(2,1)}, bf16[1024,2,2,128]{0,3,2,1:T(8,128)(2,1)S(1)}, u32[]{:S(2)}) copy-start(bf16[1024,2,2,128]{0,3,2,1:T(8,128)(2,1)S(1)} %pad_maximum_fusion.3) | copy-start | bytes 3145732
  205.7 93.6 %copy-start.59 = (f32[256]{0:T(256)S(1)}, f32[256]{0:T(256)}, u32[]{:S(2)}) copy-start(f32[256]{0:T(256)} %param.24) | copy-start | bytes 3076
  205.8 253.0 %all-gather.17.cloned.1.call-start = ((), (), s32[]{:S(2)}) async-start(), calls=%async_computation.12 | async-start | bytes 7077888 | tf_op jit(solution)/shard_map/all_gather | solution.py:158
  208.1 350.7 %all-gather.19.cloned.1.call-start = ((), (), s32[]{:S(2)}) async-start(), calls=%async_computation.13 | async-start | bytes 7077888 | tf_op jit(solution)/shard_map/all_gather | solution.py:159
  208.3 21.4 %copy-start.45 = (bf16[1536,256]{1,0:T(8,128)(2,1)}, bf16[1536,256]{1,0:T(8,128)(2,1)S(1)}, u32[]{:S(2)}) copy-start(bf16[1536,256]{1,0:T(8,128)(2,1)S(1)} %convert_element_type.250) | copy-start | bytes 2359300
  208.3 21.4 %collective-permute-start = (bf16[1536,256]{1,0:T(8,128)(2,1)S(1)}, bf16[1536,256]{1,0:T(8,128)(2,1)S(1)}, u32[]{:S(2)}, u32[]{:S(2)}) collective-permute-start(bf16[1536,256]{1,0:T(8,128)(2,1)S(1)} %convert_element_type.250), channel_id=1, source_target_pairs={{0,4},{4,8},{8,12},{12,16},{16,20},{20,24},{24,28},{28,0},{1,5},{5... | collective-permute-start | bytes 2359304 | tf_op jit(solution)/shard_map/ppermute | solution.py:24
  212.3 479.8 %all-reduce.16.cloned.1.call-start = ((), (), s32[]{:S(2)}) async-start(), calls=%async_computation.14 | async-start | bytes 8388608 | tf_op jit(solution)/shard_map/psum | solution.py:241
  229.7 32.7 %collective-permute-start.1 = (bf16[1536,256]{1,0:T(8,128)(2,1)S(1)}, bf16[1536,256]{1,0:T(8,128)(2,1)S(1)}, u32[]{:S(2)}, u32[]{:S(2)}) collective-permute-start(bf16[1536,256]{1,0:T(8,128)(2,1)S(1)} %collective-permute-done), channel_id=1, source_target_pairs={{0,4},{4,8},{8,12},{12,16},{16,20},{20,24},{24,28},{28,0},{1,5},{5... | collective-permute-start | bytes 2359304 | tf_op jit(solution)/shard_map/ppermute | solution.py:24
  229.7 35.2 %collective-permute-start.4 = (bf16[1536,256]{1,0:T(8,128)(2,1)}, bf16[1536,256]{1,0:T(8,128)(2,1)S(1)}, u32[]{:S(2)}, u32[]{:S(2)}) collective-permute-start(bf16[1536,256]{1,0:T(8,128)(2,1)} %copy-done.45), channel_id=1, source_target_pairs={{0,28},{4,0},{8,4},{12,8},{16,12},{20,16},{24,20},{28,24},{1,29},{... | collective-permute-start | bytes 2359304 | tf_op jit(solution)/shard_map/ppermute | solution.py:27
  262.4 34.4 %collective-permute-start.2 = (bf16[1536,256]{1,0:T(8,128)(2,1)S(1)}, bf16[1536,256]{1,0:T(8,128)(2,1)}, u32[]{:S(2)}, u32[]{:S(2)}) collective-permute-start(bf16[1536,256]{1,0:T(8,128)(2,1)S(1)} %collective-permute-done.1), channel_id=1, source_target_pairs={{0,4},{4,8},{8,12},{12,16},{16,20},{20,24},{24,28},{28,0},{1,5},{5... | collective-permute-start | bytes 2359304 | tf_op jit(solution)/shard_map/ppermute | solution.py:24
  264.9 65.7 %collective-permute-start.5 = (bf16[1536,256]{1,0:T(8,128)(2,1)S(1)}, bf16[1536,256]{1,0:T(8,128)(2,1)}, u32[]{:S(2)}, u32[]{:S(2)}) collective-permute-start(bf16[1536,256]{1,0:T(8,128)(2,1)S(1)} %collective-permute-done.4), channel_id=1, source_target_pairs={{0,28},{4,0},{8,4},{12,8},{16,12},{20,16},{24,20},{28,24},{1,29},{... | collective-permute-start | bytes 2359304 | tf_op jit(solution)/shard_map/ppermute | solution.py:27
  296.8 33.9 %collective-permute-start.3 = (bf16[1536,256]{1,0:T(8,128)(2,1)}, bf16[1536,256]{1,0:T(8,128)(2,1)}, u32[]{:S(2)}, u32[]{:S(2)}) collective-permute-start(bf16[1536,256]{1,0:T(8,128)(2,1)} %collective-permute-done.2), channel_id=1, source_target_pairs={{0,4},{4,8},{8,12},{12,16},{16,20},{20,24},{24,28},{28,0},{1,5},{5... | collective-permute-start | bytes 2359304 | tf_op jit(solution)/shard_map/ppermute | solution.py:24
  330.6 16.7 %collective-permute-start.6 = (bf16[1536,256]{1,0:T(8,128)(2,1)}, bf16[1536,256]{1,0:T(8,128)(2,1)S(1)}, u32[]{:S(2)}, u32[]{:S(2)}) collective-permute-start(bf16[1536,256]{1,0:T(8,128)(2,1)} %collective-permute-done.5), channel_id=1, source_target_pairs={{0,28},{4,0},{8,4},{12,8},{16,12},{20,16},{24,20},{28,24},{1,29},{... | collective-permute-start | bytes 2359304 | tf_op jit(solution)/shard_map/ppermute | solution.py:27
  335.0 17.5 %copy-start.33 = (bf16[1536,256]{1,0:T(8,128)(2,1)S(1)}, bf16[1536,256]{1,0:T(8,128)(2,1)}, u32[]{:S(2)}) copy-start(bf16[1536,256]{1,0:T(8,128)(2,1)} %copy-done.32) | copy-start | bytes 2359300
  558.8 11.9 copy-start.30
  558.8 28.1 %slice-start.10 = ((s8[6291456]{0:T(1024)(128)(4,1)}), s8[4194304]{0:T(1024)(128)(4,1)S(1)}, s32[]{:S(2)}) async-start(s8[6291456]{0:T(1024)(128)(4,1)} %bitcast.281), calls=%async_computation.33 | async-start | bytes 8388608
  570.7 16.2 %slice-start.11 = ((s8[6291456]{0:T(1024)(128)(4,1)}), s8[2097152]{0:T(1024)(128)(4,1)S(1)}, s32[]{:S(2)}) async-start(s8[6291456]{0:T(1024)(128)(4,1)} %bitcast.281), calls=%async_computation.34 | async-start | bytes 4194304
  586.9 10.6 copy-start.56
  586.9 10.6 copy-start.63
  608.2 207.9 %reduce-scatter.10.cloned.1.call-start = ((), (), s32[]{:S(2)}) async-start(), calls=%async_computation.16 | async-start | bytes 1179648 | tf_op jit(solution)/shard_map/reduce_scatter | solution.py:340
  692.1 15.5 %slice-start = ((s8[8388608]{0:T(1024)(128)(4,1)}), s8[4194304]{0:T(1024)(128)(4,1)S(1)}, s32[]{:S(2)}) async-start(s8[8388608]{0:T(1024)(128)(4,1)} %bitcast.227), calls=%async_computation.23 | async-start | bytes 8388608
  699.1 8.4 slice-start.1
  707.6 7.7 copy-start.26
  707.6 7.6 slice-start.4
  712.8 10.9 copy-start.17
  736.8 218.3 %all-reduce.18.cloned.1.call-start = ((), (), s32[]{:S(2)}) async-start(), calls=%async_computation.22 | async-start | bytes 16777216 | tf_op jit(solution)/shard_map/psum | solution.py:226
  742.7 9.6 slice-start.2
  758.5 264.3 %reduce-scatter.12.cloned.1.call-start = ((), (), s32[]{:S(2)}) async-start(), calls=%async_computation.17 | async-start | bytes 1179648 | tf_op jit(solution)/shard_map/reduce_scatter | solution.py:343
  763.5 330.8 %reduce-scatter.8.cloned.1.call-start = ((), (), s32[]{:S(2)}) async-start(), calls=%async_computation.15 | async-start | bytes 2359296 | tf_op jit(solution)/shard_map/reduce_scatter | solution.py:337
  770.3 395.4 %reduce-scatter.14.cloned.1.call-start = ((), (), s32[]{:S(2)}) async-start(), calls=%async_computation.18 | async-start | bytes 2359296 | tf_op jit(solution)/shard_map/reduce_scatter | solution.py:346
  777.5 508.9 %reduce-scatter.16.cloned.1.call-start = ((), (), s32[]{:S(2)}) async-start(), calls=%async_computation.19 | async-start | bytes 7077888 | tf_op jit(solution)/shard_map/reduce_scatter | solution.py:354
  789.1 618.3 %reduce-scatter.18.cloned.1.call-start = ((), (), s32[]{:S(2)}) async-start(), calls=%async_computation.20 | async-start | bytes 7077888 | tf_op jit(solution)/shard_map/reduce_scatter | solution.py:357
  802.0 726.9 %reduce-scatter.20.cloned.1.call-start = ((), (), s32[]{:S(2)}) async-start(), calls=%async_computation.21 | async-start | bytes 7077888 | tf_op jit(solution)/shard_map/reduce_scatter | solution.py:360
  (52 other events, 178.1 us)
Sparse Core Ops, SparseCore 0:
  10.8 42.9 all-gather.10
  56.4 39.1 all-gather.8
  98.3 48.0 all-gather.12
  148.9 49.5 all-gather.14
  205.9 151.0 all-reduce.13
  359.6 99.1 all-gather.16
  461.5 97.1 all-gather.18
  608.4 83.6 all-reduce.15
  736.9 63.4 reduce-scatter.9
  802.8 152.2 all-reduce.17
  959.1 63.7 reduce-scatter.11
  1027.2 67.0 reduce-scatter.7
  1098.3 67.3 reduce-scatter.13
  1169.5 116.8 reduce-scatter.15
  1290.3 117.1 reduce-scatter.17
  1411.3 117.4 reduce-scatter.19
